TPU v7x, 512 devices: a whole 4x4x16 slice. The times are simulated.
512 devices in a mesh: sample: 32 (over y, x, core), space: 16 (over z).
Axes of the slice: x: 4, y: 4, z: 16, core: 2. Of those that a mesh axis runs over, the one named last changes fastest.
Arguments:
- volumes: bfloat16 [32, 32, 64, 16, 128], P('sample', None, 'space'), may hold values from -360 to 360
- depth_kernel: float32 [32, 27], replicated, may hold values from -1.25 to 1.25
- point_weight: bfloat16 [32, 32], replicated, may hold values from -1 to 1
- cotangent: bfloat16 [32, 32, 64, 16, 128], P('sample', None, 'space'), may hold values from -4.1 to 4.1
Outputs:
- whitened: bfloat16 [32, 32, 64, 16, 128], P('sample', None, 'space')
- d_volumes: bfloat16 [32, 32, 64, 16, 128], P('sample', None, 'space')
- d_point: float32 [32, 32], replicated
- d_kernel: float32 [32, 27], replicated
All inputs are finite; a program needn't handle non-finite values.
Results may differ from a plain program's by a relative error of at most 0.0067.
Values may be sent and summed in bfloat16 or wider, within the bound.
No kernel may reach another device: no remote copies, remote signals or barrier semaphores. Data moves between devices by JAX's collectives and lax.ppermute only.
A program may use at most 64 MiB of HBM per device.

v0:
```python
from functools import partial
import math
import jax
import jax.numpy as jnp
from jax import lax
from jax.sharding import PartitionSpec as P

GSIZE = 16
NEWTON = 5
GROUPS = 2
epsilon = 1e-05
highest = lax.Precision.HIGHEST


def with_halo(block, sides, width):
    for axis, dim in sides:
        count = lax.axis_size(axis)
        forward = [(i, i + 1) for i in range(count - 1)]
        backward = [(target, source) for source, target in forward]
        low = lax.ppermute(
            lax.slice_in_dim(block, block.shape[dim] - width, None, axis=dim), axis, forward
        )
        high = lax.ppermute(lax.slice_in_dim(block, 0, width, axis=dim), axis, backward)
        block = jnp.concatenate([low, block, high], axis=dim)
    return block


def matmul_high(matrix, operand):
    return jnp.matmul(matrix, operand, precision=highest)


def contract_rows(matrix, operand):
    return jnp.einsum(
        "cv,dv->cd", matrix, operand, precision=highest, preferred_element_type=jnp.float32
    )


def contract_cols(matrix, operand):
    return jnp.einsum(
        "kc,kv->cv", matrix, operand, precision=highest, preferred_element_type=jnp.float32
    )


def block_diagonal(blocks):
    identity = jnp.eye(blocks.shape[0], dtype=blocks.dtype)
    full_size = blocks.shape[0] * blocks.shape[1]
    return jnp.einsum("gh,gij->gihj", identity, blocks, precision=highest).reshape(
        full_size, full_size
    )


def whiten_stats(first_sums, second_sums, voxel_count):
    groups = second_sums.shape[0]
    group_size = second_sums.shape[1]
    average = (first_sums / voxel_count).reshape(groups, group_size)
    identity = jnp.eye(group_size, dtype=second_sums.dtype)
    covariance = (
        second_sums / voxel_count - average[:, :, None] * average[:, None, :] + epsilon * identity
    )
    traces = jnp.trace(covariance, axis1=1, axis2=2)
    normed = covariance / traces[:, None, None]
    project = jnp.broadcast_to(identity, covariance.shape)
    for newton_step in range(NEWTON):
        cubed = matmul_high(matmul_high(project, project), project)
        project = 0.5 * (3.0 * project - matmul_high(cubed, normed))
    whiten_mat = project / jnp.sqrt(traces)[:, None, None]
    offset = jnp.einsum("gij,gj->gi", whiten_mat, average, precision=highest)
    return (whiten_mat, offset)


def adjoint_terms(pull_back, whiten_mat, grad_first, grad_second):
    d_first, d_second = pull_back(
        (grad_second, -grad_first.reshape(whiten_mat.shape[0], whiten_mat.shape[1]))
    )
    adjoint = block_diagonal(jnp.swapaxes(whiten_mat, 1, 2))
    symmetric = block_diagonal(d_second + jnp.swapaxes(d_second, 1, 2))
    return (d_first, adjoint, symmetric)


def gradient_signal(adjoint, d_first, symmetric, grad_part, mixed_part):
    first_term = jnp.dot(adjoint, grad_part, precision=highest, preferred_element_type=jnp.float32)
    third_term = jnp.dot(
        symmetric, mixed_part, precision=highest, preferred_element_type=jnp.float32
    )
    return first_term + d_first[:, None] + third_term


def pad_sides(extended):
    return jnp.pad(extended, ((0, 0), (0, 0), (1, 1), (1, 1)))


def tap_cells(padded, tap_index, depth_cells):
    plane_off = tap_index // 9
    row_off = tap_index // 3 % 3
    col_off = tap_index % 3
    height = padded.shape[2] - 2
    width_cells = padded.shape[3] - 2
    return padded[
        :,
        plane_off : plane_off + depth_cells,
        row_off : row_off + height,
        col_off : col_off + width_cells,
    ]


def depth_conv(extended, kernel, depth_cells):
    padded = pad_sides(extended)
    summed = jnp.zeros(
        (extended.shape[0], depth_cells, extended.shape[2], extended.shape[3]), jnp.float32
    )
    for tap_index in range(27):
        summed = summed + kernel[:, tap_index][:, None, None, None] * tap_cells(
            padded, tap_index, depth_cells
        ).astype(jnp.float32)
    return summed


def depth_adjoint(grad_ext, kernel, depth_cells):
    padded = pad_sides(grad_ext)
    height = grad_ext.shape[2]
    width_cells = grad_ext.shape[3]
    summed = jnp.zeros((grad_ext.shape[0], depth_cells, height, width_cells), jnp.float32)
    for tap_index in range(27):
        plane_off = 2 - tap_index // 9
        row_off = 2 - tap_index // 3 % 3
        col_off = 2 - tap_index % 3
        summed = (
            summed
            + kernel[:, tap_index][:, None, None, None]
            * padded[
                :,
                plane_off : plane_off + depth_cells,
                row_off : row_off + height,
                col_off : col_off + width_cells,
            ]
        )
    return summed


def on_device(volumes, depth_kernel, point_weight, cotangent):
    volume = volumes[0]
    grad_in = cotangent[0]
    channels, depth_cells, height, width_cells = volume.shape
    voxels = depth_cells * height * width_cells
    voxel_count = float(voxels * lax.axis_size("sample") * lax.axis_size("space"))
    grad_flat = grad_in.reshape(channels, voxels)
    extended = with_halo(volume, (("space", 1),), 1)
    hidden = (
        depth_conv(extended, depth_kernel, depth_cells)
        .astype(jnp.bfloat16)
        .reshape(channels, voxels)
    )
    mixed_out = jnp.dot(point_weight, hidden, preferred_element_type=jnp.float32).astype(
        jnp.bfloat16
    )
    grouped = mixed_out.reshape(GROUPS, GSIZE, voxels)
    local_first = jnp.sum(mixed_out.astype(jnp.float32), axis=1)
    local_second = jnp.einsum("giv,gjv->gij", grouped, grouped, preferred_element_type=jnp.float32)
    grad_first = jnp.sum(grad_flat.astype(jnp.float32), axis=1)
    grad_second = jnp.einsum(
        "giv,gjv->gij",
        grad_flat.reshape(GROUPS, GSIZE, voxels),
        grouped,
        preferred_element_type=jnp.float32,
    )
    padded_x = pad_sides(extended)
    weight_f = point_weight.astype(jnp.float32)
    stats_fn = partial(whiten_stats, voxel_count=voxel_count)
    first_sums, second_sums, grad_first, grad_second = lax.psum(
        (local_first, local_second, grad_first, grad_second), ("sample", "space")
    )
    (whiten_mat, offset), pull_back = jax.vjp(stats_fn, first_sums, second_sums)
    d_first, adjoint, symmetric = adjoint_terms(pull_back, whiten_mat, grad_first, grad_second)
    whitened = (
        jnp.dot(
            block_diagonal(whiten_mat),
            mixed_out,
            precision=highest,
            preferred_element_type=jnp.float32,
        )
        - offset.reshape(channels)[:, None]
    ).astype(jnp.bfloat16)
    d_mixed = gradient_signal(adjoint, d_first, symmetric, grad_flat, mixed_out)
    d_hidden = contract_cols(weight_f, d_mixed).reshape(channels, depth_cells, height, width_cells)
    grad_ext = with_halo(d_hidden, (("space", 1),), 1)
    kernel_terms = jnp.stack(
        [
            jnp.sum(
                d_hidden * tap_cells(padded_x, tap_index, depth_cells).astype(jnp.float32),
                axis=(1, 2, 3),
            )
            for tap_index in range(27)
        ],
        axis=1,
    )
    d_point, d_kernel = lax.psum(
        (contract_rows(d_mixed, hidden), kernel_terms), ("sample", "space")
    )
    d_volume = depth_adjoint(grad_ext, depth_kernel, depth_cells).astype(jnp.bfloat16)
    scale_out = 1.0 / math.sqrt(voxel_count)
    return (
        whitened.reshape(1, channels, depth_cells, height, width_cells),
        d_volume[None],
        d_point * scale_out,
        d_kernel * scale_out,
    )


def solution(mesh):
    in_specs = (
        P("sample", None, "space", None, None),
        P(),
        P(),
        P("sample", None, "space", None, None),
    )
    out_specs = (
        P("sample", None, "space", None, None),
        P("sample", None, "space", None, None),
        P(),
        P(),
    )
    return jax.shard_map(
        on_device, mesh=mesh, in_specs=in_specs, out_specs=out_specs, check_vma=False
    )
```

profile of v0, /device:TPU:1, one launch (start us, length us, event | category | flops | bytes accessed | tf_op | source)
XLA Modules:
  0.0 388.2 jit_solution(1286581559153312555)
XLA Ops:
  1.8 4.4 %collective-permute-start = (bf16[32,1,16,128]{3,2,1,0:T(8,128)(2,1)S(1)}, bf16[32,1,16,128]{3,2,1,0:T(8,128)(2,1)S(1)}, u32[]{:S(2)}, u32[]{:S(2)}) collective-permute-start(bf16[32,1,16,128]{3,2,1,0:T(8,128)(2,1)S(1)} %get-tuple-element.77), channel_id=1, source_target_pairs={{0,1},{1,2},{2,3},{3,4},{4,5},{5,6},{6,7},{7,8},{8,9},{9,10},{10,1... | collective-permute-start | bytes 393224 | tf_op jit(solution)/shard_map/ppermute | solution.py:20
  9.2 1.9 slice_reduce_fusion.25
  11.1 2.6 slice_reduce_fusion.26
  13.7 2.1 reshape_squeeze.3
  15.8 2.1 reshape_reshape_squeeze.3
  17.8 2.2 reshape.120
  22.5 3.0 select_maximum_fusion.2
  25.5 7.8 %fusion.59 = bf16[32,4,16,128]{3,2,1,0:T(8,128)(2,1)S(1)} fusion(bf16[32,4,16,128]{3,2,1,0:T(8,128)(2,1)S(1)} %bitcast.174, bf16[32,1,16,128]{3,2,1,0:T(8,128)(2,1)} %collective-permute-done.1, bf16[32,1,16,128]{3,2,1,0:T(8,128)(2,1)S(1)} %collective-permute-done, f32[32]{0:T(128)} %get-tuple-element.67, f32[32]{0:T(128)} %get-tuple-element.68, ...), kind=kLoop, calls=%fused_computation.140 | loop fusion | flops 21757952 | bytes 13897088 | tf_op jit(solution)/shard_map/convert_element_type | solution.py:150
  36.4 111.9 %all-reduce.3 = (f32[32]{0:T(128)}, f32[2,16,16]{2,1,0:T(8,128)}, f32[2,16,16]{1,2,0:T(8,128)}, f32[32]{0:T(128)}) all-reduce(f32[32]{0:T(128)} %get-tuple-element.91, f32[2,16,16]{2,1,0:T(8,128)} %fusion.215, f32[2,16,16]{1,2,0:T(8,128)} %convolution_bitcast_fusion, ...), channel_id=1, replica_groups=mesh['sample'=32,'space'=16] {'sample','space'}, use_global_device_ids=true, to_apply=%region_2.3 | all-reduce | flops 1088 | bytes 8704 | tf_op jit(solution)/shard_map/psum | solution.py:169
  162.7 1.6 fusion.212
  179.6 1.5 fusion.209
  198.2 1.6 fusion.208
  205.4 1.6 multiply_reduce_fusion.2
  209.7 1.5 multiply_reduce_fusion.3
  222.9 1.7 convolution_add_fusion.1
  228.9 6.7 %fusion.60 = (f32[32]{0:T(128)S(1)}, f32[32]{0:T(128)S(1)}, f32[32]{0:T(128)}, f32[32]{0:T(128)}, f32[32]{0:T(128)}, /*index=5*/f32[32]{0:T(128)}, f32[32]{0:T(1...) fusion(f32[32,4,16,128]{3,2,1,0:T(8,128)S(1)} %bitcast.164, ...), kind=kLoop, calls=%fused_computation.141 | loop fusion | flops 14155200 | bytes 10488064 | tf_op jit(solution)/shard_map/reduce_sum | solution.py:188
  239.8 4.3 %fusion.57 = (f32[32]{0:T(128)}, f32[32]{0:T(128)}, f32[32]{0:T(128)}, f32[32]{0:T(128)}, f32[32]{0:T(128)}, /*index=5*/f32[32]{0:T(128)}, f32[32]{0:T(128)}, f32[32]{0:T(128)}) fusion(f32[32,4,16,128]{3,2,1,0:T(8,128)S(1)} %bitcast.166, bf16[32,6,18,130]{3,2,1,0:T(8,128)(2,1)S(1)} %select_maximum_fusion.2, bf16[32,4,16,128]{3,2,1,0:T(8,128)(2,1)} %bitcast.172, ...), kind=kLoop, calls=%fused_computation.138 | loop fusion | flops 6815488 | bytes 4981760 | tf_op jit(solution)/shard_map/reduce_sum | solution.py:188
  244.4 2.8 stack.111
  247.2 99.9 %all-reduce.2 = (f32[32,32]{1,0:T(8,128)S(1)}, f32[32,27]{0,1:T(8,128)S(1)}) all-reduce(f32[32,32]{1,0:T(8,128)} %fusion.91, f32[32,27]{0,1:T(8,128)S(1)} %stack.111), channel_id=1, replica_groups=mesh['sample'=32,'space'=16] {'sample','space'}, use_global_device_ids=true, to_apply=%region_11.12 | all-reduce | flops 1888 | bytes 15104 | tf_op jit(solution)/shard_map/psum | solution.py:196
  347.1 3.3 collective-permute-start.2
  351.6 1.6 fusion.5
  355.6 3.7 collective-permute-done.3
  359.3 3.4 select_maximum_fusion
  363.0 25.1 %fusion.94 = bf16[1,32,4,16,128]{4,3,2,1,0:T(8,128)(2,1)} fusion(f32[32,6,18,130]{3,2,1,0:T(8,128)} %select_maximum_fusion, f32[32]{0:T(128)S(1)} %copy-done.23, f32[32]{0:T(128)S(1)} %copy-done.24, f32[32]{0:T(128)S(1)} %copy-done.26, f32[32]{0:T(128)S(1)} %copy-done.27, f32[32,4,16,128]{3,2,1,0:T(8,128)S(1)} %bitcast.168, ...), kind=kLoop, calls=%fused_computation.206 | loop fusion | flops 14680064 | bytes 27266432 | tf_op jit(solution)/shard_map/broadcast_in_dim | solution.py:203
  (188 shorter events, 88.7 us)
Async XLA Ops:
  1.8 20.8 %collective-permute-start = (bf16[32,1,16,128]{3,2,1,0:T(8,128)(2,1)S(1)}, bf16[32,1,16,128]{3,2,1,0:T(8,128)(2,1)S(1)}, u32[]{:S(2)}, u32[]{:S(2)}) collective-permute-start(bf16[32,1,16,128]{3,2,1,0:T(8,128)(2,1)S(1)} %get-tuple-element.77), channel_id=1, source_target_pairs={{0,1},{1,2},{2,3},{3,4},{4,5},{5,6},{6,7},{7,8},{8,9},{9,10},{10,1... | collective-permute-start | bytes 393224 | tf_op jit(solution)/shard_map/ppermute | solution.py:20
  6.1 16.4 %collective-permute-start.1 = (bf16[32,1,16,128]{3,2,1,0:T(8,128)(2,1)S(1)}, bf16[32,1,16,128]{3,2,1,0:T(8,128)(2,1)}, u32[]{:S(2)}, u32[]{:S(2)}) collective-permute-start(bf16[32,1,16,128]{3,2,1,0:T(8,128)(2,1)S(1)} %get-tuple-element.78), channel_id=1, source_target_pairs={{1,0},{2,1},{3,2},{4,3},{5,4},{6,5},{7,6},{8,7},{9,8},{10,9},{11,1... | collective-permute-start | bytes 393224 | tf_op jit(solution)/shard_map/ppermute | solution.py:23
  34.5 191.4 %copy-start.1 = (bf16[8192,32]{0,1:T(8,128)(2,1)}, bf16[8192,32]{0,1:T(8,128)(2,1)S(1)}, u32[]{:S(2)}) copy-start(bf16[8192,32]{0,1:T(8,128)(2,1)S(1)} %get-tuple-element.92) | copy-start | bytes 1572868
  244.2 118.6 %copy-start.22 = (f32[32]{0:T(128)S(1)}, f32[32]{0:T(128)}, u32[]{:S(2)}) copy-start(f32[32]{0:T(128)} %get-tuple-element.66) | copy-start | bytes 388
  244.2 118.6 %copy-start.23 = (f32[32]{0:T(128)S(1)}, f32[32]{0:T(128)}, u32[]{:S(2)}) copy-start(f32[32]{0:T(128)} %get-tuple-element.67) | copy-start | bytes 388
  244.2 118.6 %copy-start.24 = (f32[32]{0:T(128)S(1)}, f32[32]{0:T(128)}, u32[]{:S(2)}) copy-start(f32[32]{0:T(128)} %get-tuple-element.68) | copy-start | bytes 388
  244.2 118.6 %copy-start.25 = (f32[32]{0:T(128)S(1)}, f32[32]{0:T(128)}, u32[]{:S(2)}) copy-start(f32[32]{0:T(128)} %get-tuple-element.42) | copy-start | bytes 388
  244.2 118.6 %copy-start.26 = (f32[32]{0:T(128)S(1)}, f32[32]{0:T(128)}, u32[]{:S(2)}) copy-start(f32[32]{0:T(128)} %get-tuple-element.43) | copy-start | bytes 388
  244.2 118.6 %copy-start.27 = (f32[32]{0:T(128)S(1)}, f32[32]{0:T(128)}, u32[]{:S(2)}) copy-start(f32[32]{0:T(128)} %get-tuple-element.44) | copy-start | bytes 388
  244.2 118.6 %copy-start.28 = (f32[32]{0:T(128)S(1)}, f32[32]{0:T(128)}, u32[]{:S(2)}) copy-start(f32[32]{0:T(128)} %get-tuple-element.45) | copy-start | bytes 388
  244.3 118.6 %copy-start.29 = (f32[32]{0:T(128)S(1)}, f32[32]{0:T(128)}, u32[]{:S(2)}) copy-start(f32[32]{0:T(128)} %get-tuple-element.46) | copy-start | bytes 388
  244.3 118.6 %copy-start.30 = (f32[32]{0:T(128)S(1)}, f32[32]{0:T(128)}, u32[]{:S(2)}) copy-start(f32[32]{0:T(128)} %get-tuple-element.47) | copy-start | bytes 388
  244.3 118.6 %copy-start.31 = (f32[32]{0:T(128)S(1)}, f32[32]{0:T(128)}, u32[]{:S(2)}) copy-start(f32[32]{0:T(128)} %get-tuple-element.48) | copy-start | bytes 388
  244.3 118.6 %copy-start.32 = (f32[32]{0:T(128)S(1)}, f32[32]{0:T(128)}, u32[]{:S(2)}) copy-start(f32[32]{0:T(128)} %get-tuple-element.49) | copy-start | bytes 388
  244.3 118.6 %copy-start.33 = (f32[32]{0:T(128)S(1)}, f32[32]{0:T(128)}, u32[]{:S(2)}) copy-start(f32[32]{0:T(128)} %get-tuple-element.50) | copy-start | bytes 388
  244.3 118.6 %copy-start.34 = (f32[32]{0:T(128)S(1)}, f32[32]{0:T(128)}, u32[]{:S(2)}) copy-start(f32[32]{0:T(128)} %get-tuple-element.51) | copy-start | bytes 388
  244.3 118.6 %copy-start.35 = (f32[32]{0:T(128)S(1)}, f32[32]{0:T(128)}, u32[]{:S(2)}) copy-start(f32[32]{0:T(128)} %get-tuple-element.52) | copy-start | bytes 388
  244.3 118.6 %copy-start.36 = (f32[32]{0:T(128)S(1)}, f32[32]{0:T(128)}, u32[]{:S(2)}) copy-start(f32[32]{0:T(128)} %get-tuple-element.53) | copy-start | bytes 388
  244.3 118.6 %copy-start.37 = (f32[32]{0:T(128)S(1)}, f32[32]{0:T(128)}, u32[]{:S(2)}) copy-start(f32[32]{0:T(128)} %get-tuple-element.54) | copy-start | bytes 388
  244.3 118.6 %copy-start.38 = (f32[32]{0:T(128)S(1)}, f32[32]{0:T(128)}, u32[]{:S(2)}) copy-start(f32[32]{0:T(128)} %get-tuple-element.55) | copy-start | bytes 388
  244.4 118.6 %copy-start.39 = (f32[32]{0:T(128)S(1)}, f32[32]{0:T(128)}, u32[]{:S(2)}) copy-start(f32[32]{0:T(128)} %get-tuple-element.56) | copy-start | bytes 388
  244.4 118.6 %copy-start.40 = (f32[32]{0:T(128)S(1)}, f32[32]{0:T(128)}, u32[]{:S(2)}) copy-start(f32[32]{0:T(128)} %get-tuple-element.57) | copy-start | bytes 388
  347.1 8.5 %collective-permute-start.2 = (f32[32,1,16,128]{3,2,1,0:T(8,128)}, f32[32,1,16,128]{3,2,1,0:T(8,128)S(1)}, u32[]{:S(2)}, u32[]{:S(2)}) collective-permute-start(f32[32,1,16,128]{3,2,1,0:T(8,128)} %get-tuple-element.75), channel_id=1, source_target_pairs={{0,1},{1,2},{2,3},{3,4},{4,5},{5,6},{6,7},{7,8},{8,9},{9,10},{10,1... | collective-permute-start | bytes 786440 | tf_op jit(solution)/shard_map/ppermute | solution.py:20
  350.3 9.0 %collective-permute-start.3 = (f32[32,1,16,128]{3,2,1,0:T(8,128)}, f32[32,1,16,128]{3,2,1,0:T(8,128)S(1)}, u32[]{:S(2)}, u32[]{:S(2)}) collective-permute-start(f32[32,1,16,128]{3,2,1,0:T(8,128)} %get-tuple-element.76), channel_id=1, source_target_pairs={{1,0},{2,1},{3,2},{4,3},{5,4},{6,5},{7,6},{8,7},{9,8},{10,9},{11,1... | collective-permute-start | bytes 786440 | tf_op jit(solution)/shard_map/ppermute | solution.py:23
  (25 other events, 1061.6 us)
where the time goes:
time: 394 us; the launch traced here: 388 us
  blocking collectives  212 us (54%)
  other arithmetic  67.2 us (17%)
  local copies, waits for them, and re-layouts  48.5 us (12%)
  matrix products  45.2 us (11%)
  starting transfers between devices  10.2 us (3%)
    psum x1, blocking collectives, on_device(): lax.psum((local_first, local_second, grad_first, grad_second), ('sample',...  112 us
    psum x1, blocking collectives, on_device(): lax.psum((contract_rows(d_mixed, hidden), kernel_terms), ('sample', 'spac...  99.9 us
    dot_general x40, matrix products, matmul_high(): return jnp.matmul(matrix, operand, precision=highest)  33.2 us
    broadcast_in_dim x1, other arithmetic, on_device(): d_volume[None]  25.1 us
    reduce_sum x2, other arithmetic, on_device(): jnp.sum(d_hidden * tap_cells(padded_x, tap_index, depth_cells).astype(jnp...  11 us
  transfers between devices with their start and end apart: 4, of which 2 were waited for; matrix products, arithmetic and copies ran while one was open for 5% of the time, Pallas kernels for 0%

commit v1 on v0

--- a/solution.py
+++ b/solution.py
@@ -167,7 +167,7 @@
     weight_f = point_weight.astype(jnp.float32)
     stats_fn = partial(whiten_stats, voxel_count=voxel_count)
     first_sums, second_sums, grad_first, grad_second = lax.psum(
-        (local_first, local_second, grad_first, grad_second), ("sample", "space")
+        lax.psum((local_first, local_second, grad_first, grad_second), "space"), "sample"
     )
     (whiten_mat, offset), pull_back = jax.vjp(stats_fn, first_sums, second_sums)
     d_first, adjoint, symmetric = adjoint_terms(pull_back, whiten_mat, grad_first, grad_second)

time: 394 us -> 470 us (1.19)
  blocking collectives: 212 us -> 287 us
    psum x1 -> x2, blocking collectives: 112 us -> 184 us  [the longest x1 134 us: on_device(): lax.psum(lax.psum((local_first, local_second, grad_first, grad_second), '...]
  transfers between devices with their start and end apart: 4 -> 4, of which waited for: 2 -> 2; matrix products, arithmetic and copies ran while one was open for 5% -> 4% of each run, Pallas kernels for 0% -> 0%
where the time goes in v1:
time: 470 us; the launch traced here: 464 us
  blocking collectives  287 us (61%)
  other arithmetic  67.1 us (14%)
  local copies, waits for them, and re-layouts  48.5 us (10%)
  matrix products  45.2 us (10%)
  starting transfers between devices  10.6 us (2%)
    psum x1, blocking collectives, on_device(): lax.psum(lax.psum((local_first, local_second, grad_first, grad_second), '...  134 us
    psum x1, blocking collectives, on_device(): lax.psum((contract_rows(d_mixed, hidden), kernel_terms), ('sample', 'spac...  103 us
    psum x1, blocking collectives, on_device(): lax.psum((local_first, local_second, grad_first, grad_second), 'space')  50.6 us
    dot_general x40, matrix products, matmul_high(): return jnp.matmul(matrix, operand, precision=highest)  33.2 us
    broadcast_in_dim x1, other arithmetic, on_device(): d_volume[None]  25.1 us
    reduce_sum x2, other arithmetic, on_device(): jnp.sum(d_hidden * tap_cells(padded_x, tap_index, depth_cells).astype(jnp...  10.8 us
  transfers between devices with their start and end apart: 4, of which 2 were waited for; matrix products, arithmetic and copies ran while one was open for 4% of the time, Pallas kernels for 0%

profile of v1, /device:TPU:1, one launch (start us, length us, event | category | flops | bytes accessed | tf_op | source)
XLA Modules:
  0.0 463.5 jit_solution(4232659392136418412)
XLA Ops:
  1.8 4.4 collective-permute-start
  9.2 1.9 slice_reduce_fusion.25
  11.1 2.6 slice_reduce_fusion.26
  13.7 2.1 reshape_squeeze.3
  15.8 2.1 reshape_reshape_squeeze.3
  17.8 2.2 reshape.120
  22.5 3.0 select_maximum_fusion.2
  25.5 7.8 %fusion.59 = bf16[32,4,16,128]{3,2,1,0:T(8,128)(2,1)S(1)} fusion(bf16[32,4,16,128]{3,2,1,0:T(8,128)(2,1)S(1)} %bitcast.174, bf16[32,1,16,128]{3,2,1,0:T(8,128)(2,1)} %collective-permute-done.1, bf16[32,1,16,128]{3,2,1,0:T(8,128)(2,1)S(1)} %collective-permute-done, f32[32]{0:T(128)} %get-tuple-element.67, f32[32]{0:T(128)} %get-tuple-element.68, ...), kind=kLoop, calls=%fused_computation.140 | loop fusion | flops 21757952 | bytes 13897088 | tf_op jit(solution)/shard_map/convert_element_type | solution.py:150
  36.4 50.6 %all-reduce.4 = (f32[32]{0:T(128)}, f32[2,16,16]{2,1,0:T(8,128)}, f32[2,16,16]{1,2,0:T(8,128)}, f32[32]{0:T(128)}) all-reduce(f32[32]{0:T(128)} %get-tuple-element.95, f32[2,16,16]{2,1,0:T(8,128)} %fusion.215, f32[2,16,16]{1,2,0:T(8,128)} %convolution_bitcast_fusion, ...), channel_id=1, replica_groups=mesh['sample'=32,'space'=16] {'space'}, use_global_device_ids=true, to_apply=%region_3.4 | all-reduce | flops 1088 | bytes 8704 | tf_op jit(solution)/shard_map/psum | solution.py:170
  87.0 133.6 %all-reduce.3 = (f32[32]{0:T(128)}, f32[2,16,16]{2,1,0:T(8,128)}, f32[2,16,16]{1,2,0:T(8,128)}, f32[32]{0:T(128)}) all-reduce(f32[32]{0:T(128)} %get-tuple-element.75, f32[2,16,16]{2,1,0:T(8,128)} %get-tuple-element.76, f32[2,16,16]{1,2,0:T(8,128)} %get-tuple-element.77, ...), channel_id=1, replica_groups=mesh['sample'=32,'space'=16] {'sample'}, use_global_device_ids=true, to_apply=%region_4.5 | all-reduce | flops 1088 | bytes 8704 | tf_op jit(solution)/shard_map/psum | solution.py:169
  235.1 1.6 fusion.212
  270.6 1.6 fusion.208
  277.8 1.6 multiply_reduce_fusion.2
  282.2 1.5 multiply_reduce_fusion.3
  295.3 1.7 convolution_add_fusion.1
  301.4 6.5 %fusion.60 = (f32[32]{0:T(128)S(1)}, f32[32]{0:T(128)S(1)}, f32[32]{0:T(128)}, f32[32]{0:T(128)}, f32[32]{0:T(128)}, /*index=5*/f32[32]{0:T(128)}, f32[32]{0:T(1...) fusion(f32[32,4,16,128]{3,2,1,0:T(8,128)S(1)} %bitcast.164, ...), kind=kLoop, calls=%fused_computation.141 | loop fusion | flops 14155200 | bytes 10488064 | tf_op jit(solution)/shard_map/reduce_sum | solution.py:188
  312.1 4.3 fusion.57
  316.6 2.8 stack.111
  319.4 102.5 %all-reduce.2 = (f32[32,32]{1,0:T(8,128)S(1)}, f32[32,27]{0,1:T(8,128)S(1)}) all-reduce(f32[32,32]{1,0:T(8,128)} %fusion.91, f32[32,27]{0,1:T(8,128)S(1)} %stack.111), channel_id=1, replica_groups=mesh['sample'=32,'space'=16] {'sample','space'}, use_global_device_ids=true, to_apply=%region_15.16 | all-reduce | flops 1888 | bytes 15104 | tf_op jit(solution)/shard_map/psum | solution.py:196
  422.0 3.7 collective-permute-start.2
  426.9 1.6 fusion.5
  430.9 3.7 collective-permute-done.3
  434.7 3.4 select_maximum_fusion
  438.3 25.1 %fusion.94 = bf16[1,32,4,16,128]{4,3,2,1,0:T(8,128)(2,1)} fusion(f32[32,6,18,130]{3,2,1,0:T(8,128)} %select_maximum_fusion, f32[32]{0:T(128)S(1)} %copy-done.23, f32[32]{0:T(128)S(1)} %copy-done.24, f32[32]{0:T(128)S(1)} %copy-done.26, f32[32]{0:T(128)S(1)} %copy-done.27, f32[32,4,16,128]{3,2,1,0:T(8,128)S(1)} %bitcast.168, ...), kind=kLoop, calls=%fused_computation.206 | loop fusion | flops 14680064 | bytes 27266432 | tf_op jit(solution)/shard_map/broadcast_in_dim | solution.py:203
  (189 shorter events, 90.3 us)
Async XLA Ops:
  1.8 20.8 %collective-permute-start = (bf16[32,1,16,128]{3,2,1,0:T(8,128)(2,1)S(1)}, bf16[32,1,16,128]{3,2,1,0:T(8,128)(2,1)S(1)}, u32[]{:S(2)}, u32[]{:S(2)}) collective-permute-start(bf16[32,1,16,128]{3,2,1,0:T(8,128)(2,1)S(1)} %get-tuple-element.81), channel_id=1, source_target_pairs={{0,1},{1,2},{2,3},{3,4},{4,5},{5,6},{6,7},{7,8},{8,9},{9,10},{10,1... | collective-permute-start | bytes 393224 | tf_op jit(solution)/shard_map/ppermute | solution.py:20
  6.1 16.4 %collective-permute-start.1 = (bf16[32,1,16,128]{3,2,1,0:T(8,128)(2,1)S(1)}, bf16[32,1,16,128]{3,2,1,0:T(8,128)(2,1)}, u32[]{:S(2)}, u32[]{:S(2)}) collective-permute-start(bf16[32,1,16,128]{3,2,1,0:T(8,128)(2,1)S(1)} %get-tuple-element.82), channel_id=1, source_target_pairs={{1,0},{2,1},{3,2},{4,3},{5,4},{6,5},{7,6},{8,7},{9,8},{10,9},{11,1... | collective-permute-start | bytes 393224 | tf_op jit(solution)/shard_map/ppermute | solution.py:23
  34.5 263.9 %copy-start.1 = (bf16[8192,32]{0,1:T(8,128)(2,1)}, bf16[8192,32]{0,1:T(8,128)(2,1)S(1)}, u32[]{:S(2)}) copy-start(bf16[8192,32]{0,1:T(8,128)(2,1)S(1)} %get-tuple-element.96) | copy-start | bytes 1572868
  316.4 121.6 %copy-start.22 = (f32[32]{0:T(128)S(1)}, f32[32]{0:T(128)}, u32[]{:S(2)}) copy-start(f32[32]{0:T(128)} %get-tuple-element.66) | copy-start | bytes 388
  316.4 121.6 %copy-start.23 = (f32[32]{0:T(128)S(1)}, f32[32]{0:T(128)}, u32[]{:S(2)}) copy-start(f32[32]{0:T(128)} %get-tuple-element.67) | copy-start | bytes 388
  316.4 121.6 %copy-start.24 = (f32[32]{0:T(128)S(1)}, f32[32]{0:T(128)}, u32[]{:S(2)}) copy-start(f32[32]{0:T(128)} %get-tuple-element.68) | copy-start | bytes 388
  316.4 121.6 %copy-start.25 = (f32[32]{0:T(128)S(1)}, f32[32]{0:T(128)}, u32[]{:S(2)}) copy-start(f32[32]{0:T(128)} %get-tuple-element.42) | copy-start | bytes 388
  316.5 121.6 %copy-start.26 = (f32[32]{0:T(128)S(1)}, f32[32]{0:T(128)}, u32[]{:S(2)}) copy-start(f32[32]{0:T(128)} %get-tuple-element.43) | copy-start | bytes 388
  316.5 121.6 %copy-start.27 = (f32[32]{0:T(128)S(1)}, f32[32]{0:T(128)}, u32[]{:S(2)}) copy-start(f32[32]{0:T(128)} %get-tuple-element.44) | copy-start | bytes 388
  316.5 121.6 %copy-start.28 = (f32[32]{0:T(128)S(1)}, f32[32]{0:T(128)}, u32[]{:S(2)}) copy-start(f32[32]{0:T(128)} %get-tuple-element.45) | copy-start | bytes 388
  316.5 121.6 %copy-start.29 = (f32[32]{0:T(128)S(1)}, f32[32]{0:T(128)}, u32[]{:S(2)}) copy-start(f32[32]{0:T(128)} %get-tuple-element.46) | copy-start | bytes 388
  316.5 121.6 %copy-start.30 = (f32[32]{0:T(128)S(1)}, f32[32]{0:T(128)}, u32[]{:S(2)}) copy-start(f32[32]{0:T(128)} %get-tuple-element.47) | copy-start | bytes 388
  316.5 121.6 %copy-start.31 = (f32[32]{0:T(128)S(1)}, f32[32]{0:T(128)}, u32[]{:S(2)}) copy-start(f32[32]{0:T(128)} %get-tuple-element.48) | copy-start | bytes 388
  316.5 121.6 %copy-start.32 = (f32[32]{0:T(128)S(1)}, f32[32]{0:T(128)}, u32[]{:S(2)}) copy-start(f32[32]{0:T(128)} %get-tuple-element.49) | copy-start | bytes 388
  316.5 121.6 %copy-start.33 = (f32[32]{0:T(128)S(1)}, f32[32]{0:T(128)}, u32[]{:S(2)}) copy-start(f32[32]{0:T(128)} %get-tuple-element.50) | copy-start | bytes 388
  316.5 121.6 %copy-start.34 = (f32[32]{0:T(128)S(1)}, f32[32]{0:T(128)}, u32[]{:S(2)}) copy-start(f32[32]{0:T(128)} %get-tuple-element.51) | copy-start | bytes 388
  316.5 121.6 %copy-start.35 = (f32[32]{0:T(128)S(1)}, f32[32]{0:T(128)}, u32[]{:S(2)}) copy-start(f32[32]{0:T(128)} %get-tuple-element.52) | copy-start | bytes 388
  316.6 121.6 %copy-start.36 = (f32[32]{0:T(128)S(1)}, f32[32]{0:T(128)}, u32[]{:S(2)}) copy-start(f32[32]{0:T(128)} %get-tuple-element.53) | copy-start | bytes 388
  316.6 121.6 %copy-start.37 = (f32[32]{0:T(128)S(1)}, f32[32]{0:T(128)}, u32[]{:S(2)}) copy-start(f32[32]{0:T(128)} %get-tuple-element.54) | copy-start | bytes 388
  316.6 121.6 %copy-start.38 = (f32[32]{0:T(128)S(1)}, f32[32]{0:T(128)}, u32[]{:S(2)}) copy-start(f32[32]{0:T(128)} %get-tuple-element.55) | copy-start | bytes 388
  316.6 121.6 %copy-start.39 = (f32[32]{0:T(128)S(1)}, f32[32]{0:T(128)}, u32[]{:S(2)}) copy-start(f32[32]{0:T(128)} %get-tuple-element.56) | copy-start | bytes 388
  316.6 121.6 %copy-start.40 = (f32[32]{0:T(128)S(1)}, f32[32]{0:T(128)}, u32[]{:S(2)}) copy-start(f32[32]{0:T(128)} %get-tuple-element.57) | copy-start | bytes 388
  422.0 9.0 %collective-permute-start.2 = (f32[32,1,16,128]{3,2,1,0:T(8,128)}, f32[32,1,16,128]{3,2,1,0:T(8,128)S(1)}, u32[]{:S(2)}, u32[]{:S(2)}) collective-permute-start(f32[32,1,16,128]{3,2,1,0:T(8,128)} %get-tuple-element.79), channel_id=1, source_target_pairs={{0,1},{1,2},{2,3},{3,4},{4,5},{5,6},{6,7},{7,8},{8,9},{9,10},{10,1... | collective-permute-start | bytes 786440 | tf_op jit(solution)/shard_map/ppermute | solution.py:20
  425.6 9.0 %collective-permute-start.3 = (f32[32,1,16,128]{3,2,1,0:T(8,128)}, f32[32,1,16,128]{3,2,1,0:T(8,128)S(1)}, u32[]{:S(2)}, u32[]{:S(2)}) collective-permute-start(f32[32,1,16,128]{3,2,1,0:T(8,128)} %get-tuple-element.80), channel_id=1, source_target_pairs={{1,0},{2,1},{3,2},{4,3},{5,4},{6,5},{7,6},{8,7},{9,8},{10,9},{11,1... | collective-permute-start | bytes 786440 | tf_op jit(solution)/shard_map/ppermute | solution.py:23
  (25 other events, 1085.8 us)
